TPU v7x, 512 devices: a whole 4x4x16 slice. The times are simulated.
512 devices in a mesh: grp: 8 (over x, core), own: 64 (over z, y).
Axes of the slice: x: 4, y: 4, z: 16, core: 2. Of those that a mesh axis runs over, the one named last changes fastest.
Arguments:
- left: bfloat16 [32768, 128, 64], P(('grp', 'own')), may hold values from -0.75 to 0.75
- right: bfloat16 [32768, 128, 64], P(('grp', 'own')), may hold values from -0.75 to 0.75
- values: bfloat16 [32768, 128], P(('grp', 'own')), may hold values from -6 to 6
- core: bfloat16 [10240, 64, 64], P(('grp', 'own')), may hold values from -6 to 6
- tile_slice: int32 [32768], P(('grp', 'own')), may hold values from 0 to 10239, as said below
- tile_fill: int32 [32768], P(('grp', 'own')), may hold values from 64 to 128
Outputs:
- new_core: bfloat16 [10240, 64, 64], P(('grp', 'own'))
- new_left: bfloat16 [32768, 128, 64], P(('grp', 'own'))
Inputs may be any that keep to these rules, and one draw needn't show every extreme that they name: `tile_slice`: call j // 20 the block of slice j and its remainder mod 64 its class. Among the tiles of one device at most 2 have slices of one class; in every group of 64 consecutive devices some class gets exactly 2 tiles from every device of the group.
All inputs are finite; a program needn't handle non-finite values.
Results may differ from a plain program's by a relative error of at most 0.0052.
Values may be sent and summed in bfloat16 or wider, within the bound.
No kernel may reach another device: no remote copies, remote signals or barrier semaphores. Data moves between devices by JAX's collectives and lax.ppermute only.
A program may use at most 64 MiB of HBM per device.

v0:
```python
import jax
import jax.numpy as jnp
from jax import lax
from jax.sharding import PartitionSpec as P


def tile_terms(left_tiles, right_tiles, value_tiles, fill_counts, slice_tables):
    tile_rows = left_tiles.shape[1]
    projected = jnp.einsum(
        "sea,sab->seb", left_tiles, slice_tables, preferred_element_type=jnp.float32
    )
    predicted = jnp.sum(projected * right_tiles.astype(jnp.float32), axis=-1)
    live_rows = jnp.arange(tile_rows)[None, :] < fill_counts[:, None]
    residual = jnp.where(live_rows, predicted - value_tiles.astype(jnp.float32), 0.0)
    weighted = (residual[:, :, None] * left_tiles.astype(jnp.float32)).astype(jnp.bfloat16)
    return jnp.einsum("sea,seb->sab", weighted, right_tiles, preferred_element_type=jnp.float32)


def body(left, right, values, core, tile_slice, tile_fill):
    owners = lax.axis_size("own")
    groups = lax.axis_size("grp")
    tile_count, tile_rows, rank_width = left.shape
    per_device = core.shape[0]
    local_count = groups * per_device
    slot_cap = 2 * tile_count // owners
    slot_total = owners * slot_cap
    dev_block = tile_slice // per_device
    target_owner = dev_block % owners
    local_slice = dev_block // owners * per_device + tile_slice % per_device
    positions = jnp.arange(tile_count)
    same_owner = target_owner[:, None] == target_owner[None, :]
    earlier = positions[None, :] < positions[:, None]
    rank_among = jnp.sum((same_owner & earlier).astype(jnp.int32), axis=1)
    slot_of_tile = target_owner * slot_cap + rank_among
    slot_match = slot_of_tile[None, :] == jnp.arange(slot_total)[:, None]
    slot_live = jnp.any(slot_match, axis=1)
    tile_of_slot = jnp.sum(jnp.where(slot_match, positions[None, :], 0), axis=1)
    send_slice = jnp.where(slot_live, local_slice[tile_of_slot], 0)
    old_tables = lax.all_gather(core, "grp", axis=0, tiled=True)
    send_left = left[tile_of_slot]
    send_right = right[tile_of_slot]
    send_values = values[tile_of_slot]
    send_fill = jnp.where(slot_live, tile_fill[tile_of_slot], 0)
    got_left, got_right, got_values, got_slice, got_fill = (
        lax.all_to_all(send_left, "own", split_axis=0, concat_axis=0, tiled=True),
        lax.all_to_all(send_right, "own", split_axis=0, concat_axis=0, tiled=True),
        lax.all_to_all(send_values, "own", split_axis=0, concat_axis=0, tiled=True),
        lax.all_to_all(send_slice, "own", split_axis=0, concat_axis=0, tiled=True),
        lax.all_to_all(send_fill, "own", split_axis=0, concat_axis=0, tiled=True),
    )
    tile_grad = tile_terms(got_left, got_right, got_values, got_fill, old_tables[got_slice])
    selector = (got_slice[:, None] == jnp.arange(local_count)[None, :]).astype(jnp.float32)
    grad_part = jnp.dot(
        selector.T,
        tile_grad.reshape(slot_total, rank_width * rank_width),
        precision=lax.Precision.HIGHEST,
        preferred_element_type=jnp.float32,
    ).reshape(local_count, rank_width, rank_width)
    grad_whole = lax.psum(grad_part, "grp")
    new_tables = (old_tables.astype(jnp.float32) - grad_whole).astype(jnp.bfloat16)
    new_mine = lax.dynamic_slice_in_dim(
        new_tables, lax.axis_index("grp") * per_device, per_device, 0
    )
    refreshed = jnp.einsum(
        "sea,sab->seb", got_left, new_tables[got_slice], preferred_element_type=jnp.float32
    ).astype(jnp.bfloat16)
    returned = lax.all_to_all(refreshed, "own", split_axis=0, concat_axis=0, tiled=True)
    new_left = returned[slot_of_tile]
    return (new_mine, new_left)


def solution(mesh):
    return jax.shard_map(
        body,
        mesh=mesh,
        in_specs=(
            P(("grp", "own"), None, None),
            P(("grp", "own"), None, None),
            P(("grp", "own"), None),
            P(("grp", "own"), None, None),
            P(("grp", "own")),
            P(("grp", "own")),
        ),
        out_specs=(P(("grp", "own"), None, None), P(("grp", "own"), None, None)),
        check_vma=False,
    )
```

profile of v0, /device:TPU:7, one launch (start us, length us, event | category | flops | bytes accessed | tf_op | source)
XLA Modules:
  0.0 528.3 jit_solution(8652673713095691326)
XLA Ops:
  12.0 18.5 %all-to-all-start.1 = ((s32[64,2,1]{1,2,0:T(1,128)}), s32[64,2,1]{1,2,0:T(1,128)S(1)}, u32[]{:S(2)}, u32[]{:S(2)}) async-start(s32[64,2,1]{1,2,0:T(1,128)} %bitcast.4), calls=%async_computation.1 | async-start | bytes 65536 | tf_op jit(solution)/shard_map/all_to_all | solution.py:49
  31.2 12.7 %all-to-all-done.1 = s32[64,2,1]{1,2,0:T(1,128)S(1)} async-done(((s32[64,2,1]{1,2,0:T(1,128)}), s32[64,2,1]{1,2,0:T(1,128)S(1)}, u32[]{:S(2)}, u32[]{:S(2)}) %all-to-all-start.1) | async-done | bytes 544 | tf_op jit(solution)/shard_map/all_to_all | solution.py:49
  43.8 4.6 all-to-all-start
  50.6 11.4 %all-to-all-done = s32[64,2,1]{1,2,0:T(1,128)S(1)} async-done(((s32[64,2,1]{1,2,0:T(1,128)}), s32[64,2,1]{1,2,0:T(1,128)S(1)}, u32[]{:S(2)}, u32[]{:S(2)}) %all-to-all-start) | async-done | bytes 544 | tf_op jit(solution)/shard_map/all_to_all | solution.py:48
  61.9 4.7 all-to-all-start.3
  66.6 3.4 gather_fusion.2
  70.0 90.1 %all-to-all-done.3 = bf16[128,128,64]{1,2,0:T(8,128)(2,1)S(1)} async-done(((bf16[128,128,64]{1,2,0:T(8,128)(2,1)}), bf16[128,128,64]{1,2,0:T(8,128)(2,1)S(1)}, u32[]{:S(2)}, u32[]{:S(2)}) %all-to-all-start.3) | async-done | bytes 2097184 | tf_op jit(solution)/shard_map/all_to_all | solution.py:46
  161.5 10.7 %all-to-all-start.2 = ((bf16[128,128,64]{1,2,0:T(8,128)(2,1)}), bf16[128,128,64]{1,2,0:T(8,128)(2,1)S(1)}, u32[]{:S(2)}, u32[]{:S(2)}) async-start(bf16[128,128,64]{1,2,0:T(8,128)(2,1)} %gather_fusion.2), calls=%async_computation.2 | async-start | bytes 4194304 | tf_op jit(solution)/shard_map/all_to_all | solution.py:45
  176.7 34.6 %all-gather.2.cloned.1.call-done = bf16[160,64,64]{2,1,0:T(8,128)(2,1)} async-done(((bf16[20,64,64]{2,1,0:T(8,128)(2,1)}), bf16[160,64,64]{2,1,0:T(8,128)(2,1)}) %all-gather.2.cloned.1.call-update) | async-done | bytes 1310736 | tf_op jit(solution)/shard_map/all_gather | solution.py:39
  211.3 3.9 gather_fusion.3
  215.2 50.7 %all-to-all-done.2 = bf16[128,128,64]{1,2,0:T(8,128)(2,1)S(1)} async-done(((bf16[128,128,64]{1,2,0:T(8,128)(2,1)}), bf16[128,128,64]{1,2,0:T(8,128)(2,1)S(1)}, u32[]{:S(2)}, u32[]{:S(2)}) %all-to-all-start.2) | async-done | bytes 2097184 | tf_op jit(solution)/shard_map/all_to_all | solution.py:45
  265.9 11.0 %all-to-all-start.4 = ((bf16[64,2,128]{2,1,0:T(2,128)(2,1)}), bf16[64,2,128]{2,1,0:T(2,128)(2,1)S(1)}, u32[]{:S(2)}, u32[]{:S(2)}) async-start(bf16[64,2,128]{2,1,0:T(2,128)(2,1)} %bitcast.6), calls=%async_computation.4 | async-start | bytes 65536 | tf_op jit(solution)/shard_map/all_to_all | solution.py:47
  280.4 9.9 %all-to-all-done.4 = bf16[64,2,128]{2,1,0:T(2,128)(2,1)S(1)} async-done(((bf16[64,2,128]{2,1,0:T(2,128)(2,1)}), bf16[64,2,128]{2,1,0:T(2,128)(2,1)S(1)}, u32[]{:S(2)}, u32[]{:S(2)}) %all-to-all-start.4) | async-done | bytes 32800 | tf_op jit(solution)/shard_map/all_to_all | solution.py:47
  290.4 4.8 fusion
  295.2 4.8 copy.30
  299.9 5.4 %fusion.1 = f32[160,64,64]{0,2,1:T(8,128)} fusion(f32[128,64,64]{0,2,1:T(8,128)} %copy.30, s32[128]{0:T(128)S(1)} %eq.50), kind=kOutput, calls=%fused_computation.12 | convolution fusion | flops 1006653440 | bytes 4719104 | tf_op jit(solution)/shard_map/dot_general | solution.py:53
  305.3 4.9 copy.26
  310.3 75.1 %all-reduce.2.cloned.1.call-done = f32[160,64,64]{0,2,1:T(8,128)} async-done(((f32[160,64,64]{0,2,1:T(8,128)}), f32[160,64,64]{0,2,1:T(8,128)}) %all-reduce.2.cloned.1.call-update) | async-done | bytes 2621456 | tf_op jit(solution)/shard_map/psum | solution.py:59
  385.4 5.0 subtract_convert_fusion
  390.4 5.0 copy.31
  395.4 3.9 gather_fusion.6
  399.3 3.8 convolution_convert_fusion
  403.0 15.8 %all-to-all-start.5 = ((bf16[128,128,64]{1,2,0:T(8,128)(2,1)}), bf16[128,128,64]{1,2,0:T(8,128)(2,1)}, u32[]{:S(2)}, u32[]{:S(2)}) async-start(bf16[128,128,64]{1,2,0:T(8,128)(2,1)} %convolution_convert_fusion), calls=%async_computation.5 | async-start | bytes 4194304 | tf_op jit(solution)/shard_map/all_to_all | solution.py:67
  422.8 95.4 %all-to-all-done.5 = bf16[128,128,64]{1,2,0:T(8,128)(2,1)} async-done(((bf16[128,128,64]{1,2,0:T(8,128)(2,1)}), bf16[128,128,64]{1,2,0:T(8,128)(2,1)}, u32[]{:S(2)}, u32[]{:S(2)}) %all-to-all-start.5) | async-done | bytes 2097184 | tf_op jit(solution)/shard_map/all_to_all | solution.py:67
  (41 shorter events, 24.2 us)
Async XLA Ops:
  7.2 41.3 %copy-start = (bf16[64,128,64]{1,2,0:T(8,128)(2,1)S(1)}, bf16[64,128,64]{1,2,0:T(8,128)(2,1)}, u32[]{:S(2)}) copy-start(bf16[64,128,64]{1,2,0:T(8,128)(2,1)} %param.7) | copy-start | bytes 3145732
  12.0 31.9 %all-to-all-start.1 = ((s32[64,2,1]{1,2,0:T(1,128)}), s32[64,2,1]{1,2,0:T(1,128)S(1)}, u32[]{:S(2)}, u32[]{:S(2)}) async-start(s32[64,2,1]{1,2,0:T(1,128)} %bitcast.4), calls=%async_computation.1 | async-start | bytes 65536 | tf_op jit(solution)/shard_map/all_to_all | solution.py:49
  43.8 18.1 %all-to-all-start = ((s32[64,2,1]{1,2,0:T(1,128)}), s32[64,2,1]{1,2,0:T(1,128)S(1)}, u32[]{:S(2)}, u32[]{:S(2)}) async-start(s32[64,2,1]{1,2,0:T(1,128)} %bitcast.2), calls=%async_computation | async-start | bytes 65536 | tf_op jit(solution)/shard_map/all_to_all | solution.py:48
  61.9 98.2 %all-to-all-start.3 = ((bf16[128,128,64]{1,2,0:T(8,128)(2,1)}), bf16[128,128,64]{1,2,0:T(8,128)(2,1)S(1)}, u32[]{:S(2)}, u32[]{:S(2)}) async-start(bf16[128,128,64]{1,2,0:T(8,128)(2,1)} %gather_fusion.4), calls=%async_computation.3 | async-start | bytes 4194304 | tf_op jit(solution)/shard_map/all_to_all | solution.py:46
  70.0 102.9 %copy-start.3 = (bf16[64,128]{1,0:T(8,128)(2,1)S(1)}, bf16[64,128]{1,0:T(8,128)(2,1)}, u32[]{:S(2)}) copy-start(bf16[64,128]{1,0:T(8,128)(2,1)} %param.8) | copy-start | bytes 49156
  160.2 1.3 copy-start.1
  161.5 104.4 %all-to-all-start.2 = ((bf16[128,128,64]{1,2,0:T(8,128)(2,1)}), bf16[128,128,64]{1,2,0:T(8,128)(2,1)S(1)}, u32[]{:S(2)}, u32[]{:S(2)}) async-start(bf16[128,128,64]{1,2,0:T(8,128)(2,1)} %gather_fusion.2), calls=%async_computation.2 | async-start | bytes 4194304 | tf_op jit(solution)/shard_map/all_to_all | solution.py:45
  172.2 39.1 %all-gather.2.cloned.1.call-start = ((), (), s32[]{:S(2)}) async-start(), calls=%async_computation.6 | async-start | bytes 2949120 | tf_op jit(solution)/shard_map/all_gather | solution.py:39
  265.9 24.4 %all-to-all-start.4 = ((bf16[64,2,128]{2,1,0:T(2,128)(2,1)}), bf16[64,2,128]{2,1,0:T(2,128)(2,1)S(1)}, u32[]{:S(2)}, u32[]{:S(2)}) async-start(bf16[64,2,128]{2,1,0:T(2,128)(2,1)} %bitcast.6), calls=%async_computation.4 | async-start | bytes 65536 | tf_op jit(solution)/shard_map/all_to_all | solution.py:47
  276.9 108.5 %all-reduce.2.cloned.1.call-start = ((), (), s32[]{:S(2)}) async-start(), calls=%async_computation.7 | async-start | bytes 8388608 | tf_op jit(solution)/shard_map/psum | solution.py:59
  403.0 15.8 %copy-start.2 = (bf16[160,64,64]{0,2,1:T(8,128)(2,1)S(1)}, bf16[160,64,64]{0,2,1:T(8,128)(2,1)}, u32[]{:S(2)}) copy-start(bf16[160,64,64]{0,2,1:T(8,128)(2,1)} %subtract_convert_fusion) | copy-start | bytes 3932164
  403.0 115.2 %all-to-all-start.5 = ((bf16[128,128,64]{1,2,0:T(8,128)(2,1)}), bf16[128,128,64]{1,2,0:T(8,128)(2,1)}, u32[]{:S(2)}, u32[]{:S(2)}) async-start(bf16[128,128,64]{1,2,0:T(8,128)(2,1)} %convolution_convert_fusion), calls=%async_computation.5 | async-start | bytes 4194304 | tf_op jit(solution)/shard_map/all_to_all | solution.py:67
Sparse Core Ops, SparseCore 0:
  175.1 36.1 all-gather.1
  305.5 79.8 all-reduce.1
where the time goes:
time: 529 us; the launch traced here: 528 us
  waiting for transfers between devices  381 us (72%)
  starting transfers between devices  65.5 us (12%)
  local copies, waits for them, and re-layouts  43.1 us (8%)
  matrix products  17.1 us (3%)
  between operations  14.2 us (3%)
  other arithmetic  7.74 us (1%)
    all_to_all x1, waiting for transfers between devices, body(): lax.all_to_all(refreshed, 'own', split_axis=0, concat_axis=0, tiled=True)  95.4 us
    all_to_all x1, waiting for transfers between devices, body(): lax.all_to_all(send_right, 'own', split_axis=0, concat_axis=0, tiled=True)  90.1 us
    psum x1, waiting for transfers between devices, body(): grad_whole = lax.psum(grad_part, 'grp')  75.1 us
    all_to_all x1, waiting for transfers between devices, body(): lax.all_to_all(send_left, 'own', split_axis=0, concat_axis=0, tiled=True)  50.7 us
    all_gather x1, waiting for transfers between devices, body(): old_tables = lax.all_gather(core, 'grp', axis=0, tiled=True)  34.6 us
    all_to_all x1, starting transfers between devices, body(): lax.all_to_all(send_fill, 'own', split_axis=0, concat_axis=0, tiled=True)  18.5 us
    all_to_all x1, starting transfers between devices, body(): lax.all_to_all(refreshed, 'own', split_axis=0, concat_axis=0, tiled=True)  15.8 us
    all_to_all x1, waiting for transfers between devices, body(): lax.all_to_all(send_fill, 'own', split_axis=0, concat_axis=0, tiled=True)  12.7 us
  transfers between devices with their start and end apart: 8, of which 8 were waited for; matrix products, arithmetic and copies ran while one was open for 5% of the time, Pallas kernels for 0%

commit v1 on v0

--- a/solution.py
+++ b/solution.py
@@ -1,7 +1,17 @@
+import functools
 import jax
 import jax.numpy as jnp
 from jax import lax
 from jax.sharding import PartitionSpec as P
+
+
+def draw_the_pipes(xin, mesh_dim):
+    return jnp.concatenate(
+        jax.lax.all_to_all(jnp.stack([xin] * jax.lax.axis_size(mesh_dim), 0), mesh_dim, 0, 0), 0
+    )
+
+
+touch_ladders = functools.partial(draw_the_pipes, mesh_dim="grp")
 
 
 def tile_terms(left_tiles, right_tiles, value_tiles, fill_counts, slice_tables):
@@ -36,7 +46,7 @@
     slot_live = jnp.any(slot_match, axis=1)
     tile_of_slot = jnp.sum(jnp.where(slot_match, positions[None, :], 0), axis=1)
     send_slice = jnp.where(slot_live, local_slice[tile_of_slot], 0)
-    old_tables = lax.all_gather(core, "grp", axis=0, tiled=True)
+    old_tables = touch_ladders(core)
     send_left = left[tile_of_slot]
     send_right = right[tile_of_slot]
     send_values = values[tile_of_slot]

time: 529 us -> 559 us (1.057)
  local copies, waits for them, and re-layouts: 43.1 us -> 56.6 us
  starting transfers between devices: 65.5 us -> 75.6 us
    all_gather x1 -> x0, waiting for transfers between devices: 34.6 us -> none  [body(): old_tables = lax.all_gather(core, 'grp', axis=0, tiled=True)]
    all_to_all x1, waiting for transfers between devices: 50.7 us -> 82.6 us  [body(): lax.all_to_all(send_left, 'own', split_axis=0, concat_axis=0, tiled=True)]
    all_to_all x0 -> x1, waiting for transfers between devices: none -> 14 us  [draw_the_pipes(): jax.lax.all_to_all(jnp.stack([xin] * jax.lax.axis_size(mesh_dim), 0), mes...]
    unnamed x9 -> x13, local copies, waits for them, and re-layouts: 3.89 us -> 14.2 us
    all_to_all x0 -> x1, starting transfers between devices: none -> 7.71 us  [draw_the_pipes(): jax.lax.all_to_all(jnp.stack([xin] * jax.lax.axis_size(mesh_dim), 0), mes...]
    all_to_all x1, waiting for transfers between devices: 11.4 us -> 5.75 us  [body(): lax.all_to_all(send_slice, 'own', split_axis=0, concat_axis=0, tiled=True)]
  transfers between devices with their start and end apart: 8 -> 8, of which waited for: 8 -> 8; matrix products, arithmetic and copies ran while one was open for 5% -> 7% of each run, Pallas kernels for 0% -> 0%
where the time goes in v1:
time: 559 us; the launch traced here: 557 us
  waiting for transfers between devices  386 us (69%)
  starting transfers between devices  75.6 us (14%)
  local copies, waits for them, and re-layouts  56.6 us (10%)
  matrix products  17.1 us (3%)
  between operations  14.2 us (3%)
  other arithmetic  7.74 us (1%)
    all_to_all x1, waiting for transfers between devices, body(): lax.all_to_all(refreshed, 'own', split_axis=0, concat_axis=0, tiled=True)  95.4 us
    all_to_all x1, waiting for transfers between devices, body(): lax.all_to_all(send_right, 'own', split_axis=0, concat_axis=0, tiled=True)  91.3 us
    all_to_all x1, waiting for transfers between devices, body(): lax.all_to_all(send_left, 'own', split_axis=0, concat_axis=0, tiled=True)  82.6 us
    psum x1, waiting for transfers between devices, body(): grad_whole = lax.psum(grad_part, 'grp')  74.5 us
    all_to_all x1, starting transfers between devices, body(): lax.all_to_all(send_fill, 'own', split_axis=0, concat_axis=0, tiled=True)  18.5 us
    all_to_all x1, starting transfers between devices, body(): lax.all_to_all(refreshed, 'own', split_axis=0, concat_axis=0, tiled=True)  15.8 us
    unnamed x13, local copies, waits for them, and re-layouts  14.2 us
    all_to_all x1, waiting for transfers between devices, draw_the_pipes(): jax.lax.all_to_all(jnp.stack([xin] * jax.lax.axis_size(mesh_dim), 0), mes...  14 us
  transfers between devices with their start and end apart: 8, of which 8 were waited for; matrix products, arithmetic and copies ran while one was open for 7% of the time, Pallas kernels for 0%

profile of v1, /device:TPU:7, one launch (start us, length us, event | category | flops | bytes accessed | tf_op | source)
XLA Modules:
  0.0 557.4 jit_solution(3237063864005066337)
XLA Ops:
  12.0 18.5 %all-to-all-start.2 = ((s32[64,2,1]{1,2,0:T(1,128)}), s32[64,2,1]{1,2,0:T(1,128)S(1)}, u32[]{:S(2)}, u32[]{:S(2)}) async-start(s32[64,2,1]{1,2,0:T(1,128)} %bitcast.5), calls=%async_computation.2 | async-start | bytes 65536 | tf_op jit(solution)/shard_map/all_to_all | solution.py:59
  31.2 12.7 %all-to-all-done.2 = s32[64,2,1]{1,2,0:T(1,128)S(1)} async-done(((s32[64,2,1]{1,2,0:T(1,128)}), s32[64,2,1]{1,2,0:T(1,128)S(1)}, u32[]{:S(2)}, u32[]{:S(2)}) %all-to-all-start.2) | async-done | bytes 544 | tf_op jit(solution)/shard_map/all_to_all | solution.py:59
  43.8 4.6 all-to-all-start.1
  51.6 4.6 reshape.228
  56.2 5.8 %all-to-all-done.1 = s32[64,2,1]{1,2,0:T(1,128)S(1)} async-done(((s32[64,2,1]{1,2,0:T(1,128)}), s32[64,2,1]{1,2,0:T(1,128)S(1)}, u32[]{:S(2)}, u32[]{:S(2)}) %all-to-all-start.1) | async-done | bytes 544 | tf_op jit(solution)/shard_map/all_to_all | solution.py:58
  61.9 7.7 %all-to-all-start = ((bf16[8,2,40960]{2,1,0:T(2,128)(2,1)}), bf16[8,2,40960]{2,1,0:T(2,128)(2,1)S(1)}, u32[]{:S(2)}, u32[]{:S(2)}) async-start(bf16[8,2,40960]{2,1,0:T(2,128)(2,1)} %reshape.228), calls=%async_computation | async-start | bytes 2621440 | tf_op jit(solution)/shard_map/all_to_all | solution.py:10
  71.8 14.0 %all-to-all-done = bf16[8,2,40960]{2,1,0:T(2,128)(2,1)S(1)} async-done(((bf16[8,2,40960]{2,1,0:T(2,128)(2,1)}), bf16[8,2,40960]{2,1,0:T(2,128)(2,1)S(1)}, u32[]{:S(2)}, u32[]{:S(2)}) %all-to-all-start) | async-done | bytes 1310752 | tf_op jit(solution)/shard_map/all_to_all | solution.py:10
  86.8 7.8 %all-to-all-start.4 = ((bf16[128,128,64]{1,2,0:T(8,128)(2,1)}), bf16[128,128,64]{1,2,0:T(8,128)(2,1)S(1)}, u32[]{:S(2)}, u32[]{:S(2)}) async-start(bf16[128,128,64]{1,2,0:T(8,128)(2,1)} %gather_fusion.4), calls=%async_computation.4 | async-start | bytes 4194304 | tf_op jit(solution)/shard_map/all_to_all | solution.py:56
  98.0 91.3 %all-to-all-done.4 = bf16[128,128,64]{1,2,0:T(8,128)(2,1)S(1)} async-done(((bf16[128,128,64]{1,2,0:T(8,128)(2,1)}), bf16[128,128,64]{1,2,0:T(8,128)(2,1)S(1)}, u32[]{:S(2)}, u32[]{:S(2)}) %all-to-all-start.4) | async-done | bytes 2097184 | tf_op jit(solution)/shard_map/all_to_all | solution.py:56
  190.7 10.8 %all-to-all-start.3 = ((bf16[128,128,64]{1,2,0:T(8,128)(2,1)}), bf16[128,128,64]{1,2,0:T(8,128)(2,1)S(1)}, u32[]{:S(2)}, u32[]{:S(2)}) async-start(bf16[128,128,64]{1,2,0:T(8,128)(2,1)} %gather_fusion.2), calls=%async_computation.3 | async-start | bytes 4194304 | tf_op jit(solution)/shard_map/all_to_all | solution.py:55
  205.2 4.7 reshape.229
  209.9 3.9 gather_fusion.3
  213.8 82.6 %all-to-all-done.3 = bf16[128,128,64]{1,2,0:T(8,128)(2,1)S(1)} async-done(((bf16[128,128,64]{1,2,0:T(8,128)(2,1)}), bf16[128,128,64]{1,2,0:T(8,128)(2,1)S(1)}, u32[]{:S(2)}, u32[]{:S(2)}) %all-to-all-start.3) | async-done | bytes 2097184 | tf_op jit(solution)/shard_map/all_to_all | solution.py:55
  296.4 10.2 %all-to-all-start.5 = ((bf16[64,2,128]{2,1,0:T(2,128)(2,1)}), bf16[64,2,128]{2,1,0:T(2,128)(2,1)S(1)}, u32[]{:S(2)}, u32[]{:S(2)}) async-start(bf16[64,2,128]{2,1,0:T(2,128)(2,1)} %bitcast.7), calls=%async_computation.5 | async-start | bytes 65536 | tf_op jit(solution)/shard_map/all_to_all | solution.py:57
  310.1 9.9 %all-to-all-done.5 = bf16[64,2,128]{2,1,0:T(2,128)(2,1)S(1)} async-done(((bf16[64,2,128]{2,1,0:T(2,128)(2,1)}), bf16[64,2,128]{2,1,0:T(2,128)(2,1)S(1)}, u32[]{:S(2)}, u32[]{:S(2)}) %all-to-all-start.5) | async-done | bytes 32800 | tf_op jit(solution)/shard_map/all_to_all | solution.py:57
  320.1 4.8 fusion
  324.8 4.8 copy.29
  329.6 5.4 fusion.1
  335.0 4.9 copy.25
  339.9 74.5 %all-reduce.2.cloned.1.call-done = f32[160,64,64]{0,2,1:T(8,128)} async-done(((f32[160,64,64]{0,2,1:T(8,128)}), f32[160,64,64]{0,2,1:T(8,128)}) %all-reduce.2.cloned.1.call-update) | async-done | bytes 2621456 | tf_op jit(solution)/shard_map/psum | solution.py:69
  414.4 5.0 subtract_convert_fusion
  419.4 5.0 copy.30
  432.1 15.8 %all-to-all-start.6 = ((bf16[128,128,64]{1,2,0:T(8,128)(2,1)}), bf16[128,128,64]{1,2,0:T(8,128)(2,1)}, u32[]{:S(2)}, u32[]{:S(2)}) async-start(bf16[128,128,64]{1,2,0:T(8,128)(2,1)} %convolution_convert_fusion), calls=%async_computation.6 | async-start | bytes 4194304 | tf_op jit(solution)/shard_map/all_to_all | solution.py:77
  451.9 95.4 %all-to-all-done.6 = bf16[128,128,64]{1,2,0:T(8,128)(2,1)} async-done(((bf16[128,128,64]{1,2,0:T(8,128)(2,1)}), bf16[128,128,64]{1,2,0:T(8,128)(2,1)}, u32[]{:S(2)}, u32[]{:S(2)}) %all-to-all-start.6) | async-done | bytes 2097184 | tf_op jit(solution)/shard_map/all_to_all | solution.py:77
  (45 shorter events, 38.7 us)
Async XLA Ops:
  7.2 62.5 %copy-start = (bf16[64,128,64]{1,2,0:T(8,128)(2,1)S(1)}, bf16[64,128,64]{1,2,0:T(8,128)(2,1)}, u32[]{:S(2)}) copy-start(bf16[64,128,64]{1,2,0:T(8,128)(2,1)} %param.7) | copy-start | bytes 3145732
  12.0 31.9 %all-to-all-start.2 = ((s32[64,2,1]{1,2,0:T(1,128)}), s32[64,2,1]{1,2,0:T(1,128)S(1)}, u32[]{:S(2)}, u32[]{:S(2)}) async-start(s32[64,2,1]{1,2,0:T(1,128)} %bitcast.5), calls=%async_computation.2 | async-start | bytes 65536 | tf_op jit(solution)/shard_map/all_to_all | solution.py:59
  43.8 18.1 %all-to-all-start.1 = ((s32[64,2,1]{1,2,0:T(1,128)}), s32[64,2,1]{1,2,0:T(1,128)S(1)}, u32[]{:S(2)}, u32[]{:S(2)}) async-start(s32[64,2,1]{1,2,0:T(1,128)} %bitcast.3), calls=%async_computation.1 | async-start | bytes 65536 | tf_op jit(solution)/shard_map/all_to_all | solution.py:58
  61.9 23.8 %all-to-all-start = ((bf16[8,2,40960]{2,1,0:T(2,128)(2,1)}), bf16[8,2,40960]{2,1,0:T(2,128)(2,1)S(1)}, u32[]{:S(2)}, u32[]{:S(2)}) async-start(bf16[8,2,40960]{2,1,0:T(2,128)(2,1)} %reshape.228), calls=%async_computation | async-start | bytes 2621440 | tf_op jit(solution)/shard_map/all_to_all | solution.py:10
  85.8 1.1 copy-start.3
  86.8 102.6 %all-to-all-start.4 = ((bf16[128,128,64]{1,2,0:T(8,128)(2,1)}), bf16[128,128,64]{1,2,0:T(8,128)(2,1)S(1)}, u32[]{:S(2)}, u32[]{:S(2)}) async-start(bf16[128,128,64]{1,2,0:T(8,128)(2,1)} %gather_fusion.4), calls=%async_computation.4 | async-start | bytes 4194304 | tf_op jit(solution)/shard_map/all_to_all | solution.py:56
  98.0 103.4 %copy-start.4 = (bf16[64,128]{1,0:T(8,128)(2,1)S(1)}, bf16[64,128]{1,0:T(8,128)(2,1)}, u32[]{:S(2)}) copy-start(bf16[64,128]{1,0:T(8,128)(2,1)} %param.8) | copy-start | bytes 49156
  189.4 1.3 copy-start.1
  190.7 105.7 %all-to-all-start.3 = ((bf16[128,128,64]{1,2,0:T(8,128)(2,1)}), bf16[128,128,64]{1,2,0:T(8,128)(2,1)S(1)}, u32[]{:S(2)}, u32[]{:S(2)}) async-start(bf16[128,128,64]{1,2,0:T(8,128)(2,1)} %gather_fusion.2), calls=%async_computation.3 | async-start | bytes 4194304 | tf_op jit(solution)/shard_map/all_to_all | solution.py:55
  296.4 23.6 %all-to-all-start.5 = ((bf16[64,2,128]{2,1,0:T(2,128)(2,1)}), bf16[64,2,128]{2,1,0:T(2,128)(2,1)S(1)}, u32[]{:S(2)}, u32[]{:S(2)}) async-start(bf16[64,2,128]{2,1,0:T(2,128)(2,1)} %bitcast.7), calls=%async_computation.5 | async-start | bytes 65536 | tf_op jit(solution)/shard_map/all_to_all | solution.py:57
  306.6 107.8 %all-reduce.2.cloned.1.call-start = ((), (), s32[]{:S(2)}) async-start(), calls=%async_computation.7 | async-start | bytes 8388608 | tf_op jit(solution)/shard_map/psum | solution.py:69
  432.1 15.8 %copy-start.2 = (bf16[160,64,64]{0,2,1:T(8,128)(2,1)S(1)}, bf16[160,64,64]{0,2,1:T(8,128)(2,1)}, u32[]{:S(2)}) copy-start(bf16[160,64,64]{0,2,1:T(8,128)(2,1)} %subtract_convert_fusion) | copy-start | bytes 3932164
  432.1 115.2 %all-to-all-start.6 = ((bf16[128,128,64]{1,2,0:T(8,128)(2,1)}), bf16[128,128,64]{1,2,0:T(8,128)(2,1)}, u32[]{:S(2)}, u32[]{:S(2)}) async-start(bf16[128,128,64]{1,2,0:T(8,128)(2,1)} %convolution_convert_fusion), calls=%async_computation.6 | async-start | bytes 4194304 | tf_op jit(solution)/shard_map/all_to_all | solution.py:77
Sparse Core Ops, SparseCore 0:
  335.2 79.2 all-reduce.1
